TPU v7x, 512 devices: a whole 4x8x8 slice. The times are simulated.
512 devices in a mesh: chain: 32 (over x_hi, z, core), term: 16 (over y, x_lo).
Axes of the slice: x: 4 (x_hi: 2, x_lo: 2; x = x_hi * 2 + x_lo), y: 8, z: 8, core: 2. Of those that a mesh axis runs over, the one named last changes fastest.
Arguments:
- wavefunction: bfloat16 [32, 4, 256, 256], P('chain')
- left_ops: bfloat16 [32, 128, 256, 256], P('chain', 'term')
- right_ops: bfloat16 [32, 128, 256, 256], P('chain', 'term')
- term_table: int32 [4, 32, 512], P(None, 'chain', 'term'), may hold values from 0 to 7, as said below
- coefficients: float32 [32, 512], P('chain', 'term'), may hold values from -0.1 to 0.3
- term_counts: int32 [32, 16], P('chain', 'term'), may hold values from 1 to 32, as said below
Outputs:
- first_hamiltonian_image: bfloat16 [32, 4, 256, 256], P('chain', None, 'term')
- second_image: bfloat16 [32, 4, 256, 256], P('chain', None, 'term')
Inputs may be any that keep to these rules, and one draw needn't show every extreme that they name: `term_table`: row 0 and 1 (source and target block) lie in 0 to 3, rows 2 and 3 (operator indices) in 0 to 7. `term_counts`: in every bond at least one term device has all 32 slots live.
All inputs are finite; a program needn't handle non-finite values.
Results may differ from a plain program's by a relative error of at most 0.014.
Values may be sent and summed in bfloat16 or wider, within the bound.
No kernel may reach another device: no remote copies, remote signals or barrier semaphores. Data moves between devices by JAX's collectives and lax.ppermute only.
A program may use at most 64 MiB of HBM per device.

v0:
```python
import jax
import jax.numpy as jnp
from jax import lax
from jax.sharding import PartitionSpec as P

epsilon = 1e-06


def shifted(value, axis, steps):
    count = lax.axis_size(axis)
    pairs = [(source, (source + steps) % count) for source in range(count)]
    return lax.ppermute(value, axis, pairs)


def apply_terms(blocks, left_blocks, right_blocks, term_rows, coef_rows, live_count):
    block_count = blocks.shape[0]
    slot_count = term_rows.shape[1]
    source = term_rows[0]
    target = term_rows[1]
    left_selection = left_blocks[term_rows[2]]
    right_selection = right_blocks[term_rows[3]]
    selected_blocks = blocks[source]
    inner_contraction = jnp.einsum(
        "skh,shu->sku", left_selection, selected_blocks, preferred_element_type=jnp.float32
    ).astype(jnp.bfloat16)
    outer_contraction = jnp.einsum(
        "lbe,leu->lbu", inner_contraction, right_selection, preferred_element_type=jnp.float32
    )
    live_mask = jnp.arange(slot_count, dtype=jnp.int32) < live_count
    weights = jnp.where(live_mask, coef_rows, jnp.float32(0.0))
    routing = (target[None, :] == jnp.arange(block_count, dtype=jnp.int32)[:, None]).astype(
        jnp.float32
    ) * weights[None, :]
    return jnp.einsum("kt,tad->kad", routing, outer_contraction, precision=lax.Precision.HIGHEST)


def body(wavefunction, left_ops, right_ops, term_table, coefficients, term_counts):
    blocks = wavefunction[0]
    neighbour = shifted(right_ops, "chain", -1)
    term_rows = term_table[:, 0, :]
    coef_rows = coefficients[0]
    live_count = term_counts[0, 0]
    left_blocks = left_ops[0]
    right_blocks = neighbour[0]
    first_part = apply_terms(blocks, left_blocks, right_blocks, term_rows, coef_rows, live_count)
    term_parts = lax.axis_size("term")
    row_count = blocks.shape[1] // term_parts
    starting_row = lax.axis_index("term") * row_count
    entry_count = float(blocks.shape[0] * blocks.shape[1] * blocks.shape[2])
    wave_f32 = blocks.astype(jnp.float32)
    wave_norm = jnp.sum(wave_f32 * wave_f32) / entry_count + epsilon
    first = lax.psum(first_part, "term")
    rayleigh = jnp.sum(wave_f32 * first) / entry_count / wave_norm
    residual = first - rayleigh * wave_f32
    direction = (residual * lax.rsqrt(jnp.sum(residual * residual) / entry_count + epsilon)).astype(
        jnp.bfloat16
    )
    second_part = apply_terms(
        direction, left_blocks, right_blocks, term_rows, coef_rows, live_count
    )
    second = lax.psum(second_part.astype(jnp.bfloat16), "term").astype(jnp.float32)
    first_rows = lax.dynamic_slice_in_dim(first, starting_row, row_count, 1)
    second_rows = lax.dynamic_slice_in_dim(second, starting_row, row_count, 1)
    return (first_rows[None].astype(jnp.bfloat16), second_rows[None].astype(jnp.bfloat16))


def solution(mesh):
    in_specs = (
        P("chain", None, None, None),
        P("chain", "term", None, None),
        P("chain", "term", None, None),
        P(None, "chain", "term"),
        P("chain", "term"),
        P("chain", "term"),
    )
    out_specs = (P("chain", None, "term", None), P("chain", None, "term", None))
    return jax.shard_map(body, mesh=mesh, in_specs=in_specs, out_specs=out_specs, check_vma=False)
```

profile of v0, /device:TPU:2, one launch (start us, length us, event | category | flops | bytes accessed | tf_op | source)
XLA Modules:
  0.0 389.5 jit_solution(7426124249693122728)
XLA Ops:
  7.2 0.0 copy-start
  7.2 0.0 all-reduce.3.cloned.1.call-start
  7.2 12.1 %collective-permute-start = (bf16[1,8,256,256]{3,2,1,0:T(8,128)(2,1)}, bf16[1,8,256,256]{3,2,1,0:T(8,128)(2,1)S(1)}, u32[]{:S(2)}, u32[]{:S(2)}) collective-permute-start(bf16[1,8,256,256]{3,2,1,0:T(8,128)(2,1)} %param.8), channel_id=1, source_target_pairs={{0,496},{16,0},{32,16},{48,32},{64,48},{80,64},{96,80},{112,96},{1... | collective-permute-start | bytes 3145736 | tf_op jit(solution)/shard_map/ppermute | solution.py:12
  20.0 1.5 copy.33
  21.4 0.1 copy.12
  21.5 0.7 fusion.32
  22.2 2.7 gather_fusion.1
  24.9 0.0 copy-done
  24.9 0.0 copy-start.2
  25.0 2.8 gather_fusion
  27.7 0.7 slice_bitcast_fusion
  28.4 0.0 copy-done.2
  28.4 3.5 collective-permute-done
  31.9 2.8 gather_fusion.2
  34.7 10.2 %fusion.6 = f32[32,256,256]{2,1,0:T(8,128)} fusion(bf16[32,256,256]{2,1,0:T(8,128)(2,1)} %gather_fusion.2, bf16[32,256,256]{2,1,0:T(8,128)(2,1)} %gather_fusion, bf16[32,256,256]{2,1,0:T(8,128)(2,1)} %gather_fusion.1), kind=kOutput, calls=%fused_computation.10 | convolution fusion | flops 2149580800 | bytes 20971520 | tf_op jit(solution)/shard_map/lbe,leu->lbu/dot_general | solution.py:26
  45.0 0.0 copy-start.1
  45.0 13.2 %fusion.2 = f32[4,256,256]{2,0,1:T(4,128)} fusion(f32[32,256,256]{2,1,0:T(8,128)} %fusion.6, f32[32]{0:T(128)S(1)} %fusion.30, s32[32]{0:T(128)S(1)} %slice_bitcast_fusion), kind=kOutput, calls=%fused_computation.6 | convolution fusion | flops 100663552 | bytes 9437440 | tf_op jit(solution)/shard_map/kt,tad->kad/dot_general | solution.py:34
  58.1 0.0 all-reduce.3.cloned.1.call-update
  58.2 0.2 all-reduce.5.cloned.1.call-start
  58.4 144.4 %all-reduce.3.cloned.1.call-done = f32[4,256,256]{2,0,1:T(4,128)} async-done(((f32[4,256,256]{2,0,1:T(4,128)}), f32[4,256,256]{2,0,1:T(4,128)}) %all-reduce.3.cloned.1.call-update) | async-done | bytes 1048592 | tf_op jit(solution)/shard_map/psum | solution.py:52
  202.8 0.0 copy-done.1
  202.8 2.4 fusion.16
  206.6 2.4 multiply_reduce_fusion
  209.6 1.7 multiply_convert_fusion
  211.4 0.1 copy.13
  211.4 2.7 gather_fusion.3
  214.2 10.2 %fusion.4 = f32[32,256,256]{2,1,0:T(8,128)} fusion(bf16[32,256,256]{2,1,0:T(8,128)(2,1)} %gather_fusion.2, bf16[32,256,256]{2,1,0:T(8,128)(2,1)} %gather_fusion, bf16[32,256,256]{2,1,0:T(8,128)(2,1)} %gather_fusion.3), kind=kOutput, calls=%fused_computation.8 | convolution fusion | flops 2149580800 | bytes 20971520 | tf_op jit(solution)/shard_map/lbe,leu->lbu/dot_general | solution.py:26
  224.4 13.0 %fusion.12 = bf16[4,256,256]{2,0,1:T(4,128)(2,1)} fusion(f32[32,256,256]{2,1,0:T(8,128)} %fusion.4, f32[32]{0:T(128)S(1)} %fusion.30, s32[32]{0:T(128)S(1)} %slice_bitcast_fusion), kind=kOutput, calls=%fused_computation.17 | convolution fusion | flops 100925696 | bytes 8913152 | tf_op jit(solution)/shard_map/kt,tad->kad/dot_general | solution.py:34
  237.4 0.0 all-reduce.5.cloned.1.call-update
  237.4 0.9 fusion.18
  238.3 0.6 copy.14
  238.9 142.4 %all-reduce.5.cloned.1.call-done = bf16[4,256,256]{2,0,1:T(4,128)(2,1)} async-done(((bf16[4,256,256]{2,0,1:T(4,128)(2,1)}), bf16[4,256,256]{2,0,1:T(4,128)(2,1)}) %all-reduce.5.cloned.1.call-update) | async-done | bytes 524304 | tf_op jit(solution)/shard_map/psum | solution.py:61
  381.3 0.8 fusion.19
  382.1 0.6 copy.15
  (3 shorter events, 0.0 us)
Async XLA Ops:
  7.2 17.8 %copy-start = (bf16[1,8,256,256]{3,2,1,0:T(8,128)(2,1)S(1)}, bf16[1,8,256,256]{3,2,1,0:T(8,128)(2,1)}, u32[]{:S(2)}) copy-start(bf16[1,8,256,256]{3,2,1,0:T(8,128)(2,1)} %param.7) | copy-start | bytes 3145732
  7.2 195.6 %all-reduce.3.cloned.1.call-start = ((), (), s32[]{:S(2)}) async-start(), calls=%async_computation | async-start | bytes 2097152 | tf_op jit(solution)/shard_map/psum | solution.py:52
  7.2 24.7 %collective-permute-start = (bf16[1,8,256,256]{3,2,1,0:T(8,128)(2,1)}, bf16[1,8,256,256]{3,2,1,0:T(8,128)(2,1)S(1)}, u32[]{:S(2)}, u32[]{:S(2)}) collective-permute-start(bf16[1,8,256,256]{3,2,1,0:T(8,128)(2,1)} %param.8), channel_id=1, source_target_pairs={{0,496},{16,0},{32,16},{48,32},{64,48},{80,64},{96,80},{112,96},{1... | collective-permute-start | bytes 3145736 | tf_op jit(solution)/shard_map/ppermute | solution.py:12
  24.9 3.4 copy-start.2
  45.0 157.9 %copy-start.1 = (bf16[1,4,256,256]{3,2,1,0:T(8,128)(2,1)S(1)}, bf16[1,4,256,256]{3,2,1,0:T(8,128)(2,1)}, u32[]{:S(2)}) copy-start(bf16[1,4,256,256]{3,2,1,0:T(8,128)(2,1)} %param.6) | copy-start | bytes 1572868
  58.2 323.1 %all-reduce.5.cloned.1.call-start = ((), (), s32[]{:S(2)}) async-start(), calls=%async_computation.1 | async-start | bytes 1048576 | tf_op jit(solution)/shard_map/psum | solution.py:61
Sparse Core Ops, SparseCore 0:
  58.3 144.4 all-reduce.2
  237.6 143.6 all-reduce.4
where the time goes:
time: 390 us
  waiting for transfers between devices  290 us (74%)
  matrix products  46.7 us (12%)
  between operations  16.8 us (4%)
  local copies, waits for them, and re-layouts  15.4 us (4%)
  starting transfers between devices  12.3 us (3%)
  other arithmetic  7.98 us (2%)
    psum x1, waiting for transfers between devices, body(): first = lax.psum(first_part, 'term')  144 us
    psum x1, waiting for transfers between devices, body(): lax.psum(second_part.astype(jnp.bfloat16), 'term').astype(jnp.float32)  142 us
    dot_general x2, matrix products, apply_terms(): jnp.einsum('kt,tad->kad', routing, outer_contraction, precision=lax.Preci...  26.2 us
    dot_general x2, matrix products, apply_terms(): jnp.einsum('lbe,leu->lbu', inner_contraction, right_selection, preferred_...  20.5 us
    ppermute x1, starting transfers between devices, shifted(): return lax.ppermute(value, axis, pairs)  12.1 us
  transfers between devices with their start and end apart: 3, of which 3 were waited for; matrix products, arithmetic and copies ran while one was open for 3% of the time, Pallas kernels for 0%

commit v1 on v0

--- a/solution.py
+++ b/solution.py
@@ -35,6 +35,10 @@
 
 
 def body(wavefunction, left_ops, right_ops, term_table, coefficients, term_counts):
+
+    def run_racks(xx, link_axis):
+        return lax.all_gather(xx, link_axis).sum(axis=0)
+
     blocks = wavefunction[0]
     neighbour = shifted(right_ops, "chain", -1)
     term_rows = term_table[:, 0, :]
@@ -49,7 +53,7 @@
     entry_count = float(blocks.shape[0] * blocks.shape[1] * blocks.shape[2])
     wave_f32 = blocks.astype(jnp.float32)
     wave_norm = jnp.sum(wave_f32 * wave_f32) / entry_count + epsilon
-    first = lax.psum(first_part, "term")
+    first = run_racks(first_part, "term")
     rayleigh = jnp.sum(wave_f32 * first) / entry_count / wave_norm
     residual = first - rayleigh * wave_f32
     direction = (residual * lax.rsqrt(jnp.sum(residual * residual) / entry_count + epsilon)).astype(

time: 390 us -> 607 us (1.56)
  waiting for transfers between devices: 290 us -> 506 us
    all_gather x0 -> x1, waiting for transfers between devices: none -> 352 us  [run_racks(): return lax.all_gather(xx, link_axis).sum(axis=0)]
    psum x1 -> x0, waiting for transfers between devices: 144 us -> none  [body(): first = lax.psum(first_part, 'term')]
    psum x1, waiting for transfers between devices: 142 us -> 150 us  [body(): lax.psum(second_part.astype(jnp.bfloat16), 'term').astype(jnp.float32)]
    reduce_sum x0 -> x1, other arithmetic: none -> 7.04 us  [run_racks(): return lax.all_gather(xx, link_axis).sum(axis=0)]
  transfers between devices with their start and end apart: 3 -> 3, of which waited for: 3 -> 3; matrix products, arithmetic and copies ran while one was open for 3% -> 1% of each run, Pallas kernels for 0% -> 0%
where the time goes in v1:
time: 607 us
  waiting for transfers between devices  506 us (83%)
  matrix products  45.8 us (8%)
  between operations  16.8 us (3%)
  local copies, waits for them, and re-layouts  15.4 us (3%)
  starting transfers between devices  12.3 us (2%)
  other arithmetic  10.5 us (2%)
    all_gather x1, waiting for transfers between devices, run_racks(): return lax.all_gather(xx, link_axis).sum(axis=0)  352 us
    psum x1, waiting for transfers between devices, body(): lax.psum(second_part.astype(jnp.bfloat16), 'term').astype(jnp.float32)  150 us
    dot_general x2, matrix products, apply_terms(): jnp.einsum('kt,tad->kad', routing, outer_contraction, precision=lax.Preci...  25.3 us
    dot_general x2, matrix products, apply_terms(): jnp.einsum('lbe,leu->lbu', inner_contraction, right_selection, preferred_...  20.5 us
  transfers between devices with their start and end apart: 3, of which 3 were waited for; matrix products, arithmetic and copies ran while one was open for 1% of the time, Pallas kernels for 0%

profile of v1, /device:TPU:2, one launch (start us, length us, event | category | flops | bytes accessed | tf_op | source)
XLA Modules:
  0.0 607.1 jit_solution(9382430547656041705)
XLA Ops:
  7.2 0.0 copy-start
  7.2 0.0 all-gather.3.cloned.1.call-start
  7.2 12.1 %collective-permute-start = (bf16[1,8,256,256]{3,2,1,0:T(8,128)(2,1)}, bf16[1,8,256,256]{3,2,1,0:T(8,128)(2,1)S(1)}, u32[]{:S(2)}, u32[]{:S(2)}) collective-permute-start(bf16[1,8,256,256]{3,2,1,0:T(8,128)(2,1)} %param.8), channel_id=1, source_target_pairs={{0,496},{16,0},{32,16},{48,32},{64,48},{80,64},{96,80},{112,96},{1... | collective-permute-start | bytes 3145736 | tf_op jit(solution)/shard_map/ppermute | solution.py:12
  20.0 0.7 fusion.31
  20.7 3.8 gather_fusion.1
  24.5 0.0 copy-done
  24.5 0.0 copy-start.2
  24.5 2.8 gather_fusion
  27.3 0.7 slice_bitcast_fusion
  28.0 0.0 copy-done.2
  28.0 4.0 collective-permute-done
  31.9 2.7 gather_fusion.2
  34.7 10.2 %fusion.6 = f32[32,256,256]{2,1,0:T(8,128)} fusion(bf16[32,256,256]{2,1,0:T(8,128)(2,1)} %gather_fusion.2, bf16[32,256,256]{2,1,0:T(8,128)(2,1)} %gather_fusion, bf16[32,256,256]{2,1,0:T(8,128)(2,1)} %gather_fusion.1), kind=kOutput, calls=%fused_computation.10 | convolution fusion | flops 2149580800 | bytes 20971520 | tf_op jit(solution)/shard_map/lbe,leu->lbu/dot_general | solution.py:26
  44.9 12.3 %fusion.2 = f32[4,256,256]{2,0,1:T(4,128)S(1)} fusion(f32[32,256,256]{2,1,0:T(8,128)} %fusion.6, f32[32]{0:T(128)S(1)} %fusion.29, s32[32]{0:T(128)S(1)} %slice_bitcast_fusion), kind=kOutput, calls=%fused_computation.6 | convolution fusion | flops 100663552 | bytes 9437440 | tf_op jit(solution)/shard_map/kt,tad->kad/dot_general | solution.py:34
  57.2 1.3 copy.15
  58.5 0.0 all-gather.3.cloned.1.call-update
  58.5 0.2 all-reduce.2.cloned.1.call-start
  58.7 352.1 %all-gather.3.cloned.1.call-done = f32[64,256,256]{2,1,0:T(8,128)} async-done(((f32[4,256,256]{2,1,0:T(8,128)}), f32[64,256,256]{2,1,0:T(8,128)}) %all-gather.3.cloned.1.call-update) | async-done | bytes 16777232 | tf_op jit(solution)/shard_map/all_gather | solution.py:40
  410.8 0.0 copy-start.1
  410.8 7.0 %reduce_sum.36 = f32[4,256,256]{2,1,0:T(8,128)S(1)} reduce(f32[16,4,256,256]{3,2,1,0:T(8,128)} %bitcast.44, f32[]{:T(128)} %constant.9.clone.1), dimensions={0}, to_apply=%region_0.1 | reduce | flops 3932160 | bytes 17825796 | tf_op jit(solution)/shard_map/reduce_sum | solution.py:40
  417.8 0.0 copy-done.1
  417.8 0.9 fusion.16
  420.1 0.9 multiply_reduce_fusion
  421.6 0.2 multiply_convert_fusion
  421.8 2.8 gather_fusion.3
  424.6 10.2 %fusion.4 = f32[32,256,256]{2,1,0:T(8,128)} fusion(bf16[32,256,256]{2,1,0:T(8,128)(2,1)} %gather_fusion.2, bf16[32,256,256]{2,1,0:T(8,128)(2,1)} %gather_fusion, bf16[32,256,256]{2,1,0:T(8,128)(2,1)} %gather_fusion.3), kind=kOutput, calls=%fused_computation.8 | convolution fusion | flops 2149580800 | bytes 20971520 | tf_op jit(solution)/shard_map/lbe,leu->lbu/dot_general | solution.py:26
  434.9 13.0 %fusion.12 = bf16[4,256,256]{2,0,1:T(4,128)(2,1)} fusion(f32[32,256,256]{2,1,0:T(8,128)} %fusion.4, f32[32]{0:T(128)S(1)} %fusion.29, s32[32]{0:T(128)S(1)} %slice_bitcast_fusion), kind=kOutput, calls=%fused_computation.17 | convolution fusion | flops 100925696 | bytes 8913152 | tf_op jit(solution)/shard_map/kt,tad->kad/dot_general | solution.py:34
  447.8 0.0 all-reduce.2.cloned.1.call-update
  447.9 0.6 copy.20
  448.5 150.4 %all-reduce.2.cloned.1.call-done = bf16[4,256,256]{2,0,1:T(4,128)(2,1)} async-done(((bf16[4,256,256]{2,0,1:T(4,128)(2,1)}), bf16[4,256,256]{2,0,1:T(4,128)(2,1)}) %all-reduce.2.cloned.1.call-update) | async-done | bytes 524304 | tf_op jit(solution)/shard_map/psum | solution.py:65
  598.9 0.8 fusion.18
  599.7 0.6 copy.21
  (5 shorter events, 0.0 us)
Async XLA Ops:
  7.2 17.3 %copy-start = (bf16[1,8,256,256]{3,2,1,0:T(8,128)(2,1)S(1)}, bf16[1,8,256,256]{3,2,1,0:T(8,128)(2,1)}, u32[]{:S(2)}) copy-start(bf16[1,8,256,256]{3,2,1,0:T(8,128)(2,1)} %param.7) | copy-start | bytes 3145732
  7.2 403.6 %all-gather.3.cloned.1.call-start = ((), (), s32[]{:S(2)}) async-start(), calls=%async_computation.1 | async-start | bytes 17825792 | tf_op jit(solution)/shard_map/all_gather | solution.py:40
  7.2 24.7 %collective-permute-start = (bf16[1,8,256,256]{3,2,1,0:T(8,128)(2,1)}, bf16[1,8,256,256]{3,2,1,0:T(8,128)(2,1)S(1)}, u32[]{:S(2)}, u32[]{:S(2)}) collective-permute-start(bf16[1,8,256,256]{3,2,1,0:T(8,128)(2,1)} %param.8), channel_id=1, source_target_pairs={{0,496},{16,0},{32,16},{48,32},{64,48},{80,64},{96,80},{112,96},{1... | collective-permute-start | bytes 3145736 | tf_op jit(solution)/shard_map/ppermute | solution.py:12
  24.5 3.5 copy-start.2
  58.5 540.4 %all-reduce.2.cloned.1.call-start = ((), (), s32[]{:S(2)}) async-start(), calls=%async_computation | async-start | bytes 1048576 | tf_op jit(solution)/shard_map/psum | solution.py:65
  410.8 7.0 %copy-start.1 = (bf16[1,4,256,256]{3,2,1,0:T(8,128)(2,1)S(1)}, bf16[1,4,256,256]{3,2,1,0:T(8,128)(2,1)}, u32[]{:S(2)}) copy-start(bf16[1,4,256,256]{3,2,1,0:T(8,128)(2,1)} %param.6) | copy-start | bytes 1572868
Sparse Core Ops, SparseCore 0:
  58.6 352.1 all-gather.2
  448.0 150.8 all-reduce.1
